TPU v7x, 256 devices: a whole 4x4x8 slice. The times are simulated.
256 devices in a mesh: box: 32 (over x, z), pencil: 8 (over y, core).
Axes of the slice: x: 4, y: 4, z: 8, core: 2. Of those that a mesh axis runs over, the one named last changes fastest.
Arguments:
- previous: bfloat16 [32, 256, 256, 128], P('box', 'pencil'), may hold values from -48 to 48
- source: bfloat16 [32, 256, 256, 128], P('box', 'pencil'), may hold values from -48 to 48
- neighbor: int32 [32, 2, 16], replicated, may hold values from 0 to 31, as said below
- depth: int32 [32, 2, 16], replicated, may hold values from 1 to 8
- wall: int32 [32, 2, 256], P('box', None, 'pencil'), may hold values 0 or 1
Outputs:
- solution: float32 [32, 256, 256, 128], P('box', 'pencil')
Inputs may be any that keep to these rules, and one draw needn't show every extreme that they name: For each face and segment, neighbor[:, face, segment] is a permutation of the 32 boxes in which no box names itself.
All inputs are finite; a program needn't handle non-finite values. No bound on the sum of `wall` on one device may be relied on, other than what follows from the above.
Results may differ from a plain program's by a relative error of at most 0.014.
Values may be sent and summed in bfloat16 or wider, within the bound.
A program may use at most 64 MiB of HBM per device.

v0:
```python
import jax
import jax.numpy as jnp
from jax import lax
from jax.sharding import PartitionSpec as P

W = 8
ITERS = 2
REFLECT = 0.6
TIMESTEP = 64.0


def sine_table(length):
    ordinal = jnp.arange(length, dtype=jnp.float32) + 1.0
    phase_angle = jnp.pi * ordinal[:, None] * ordinal[None, :] / (length + 1.0)
    return (jnp.sqrt(2.0 / (length + 1.0)) * jnp.sin(phase_angle)).astype(jnp.bfloat16)


def eigen_values(length):
    ordinal = jnp.arange(length, dtype=jnp.float32) + 1.0
    return 2.0 - 2.0 * jnp.cos(jnp.pi * ordinal / (length + 1.0))


def shards(previous, source, neighbor, depth, wall):
    pencils = lax.axis_size("pencil")
    pencil_index = lax.axis_index("pencil")
    box_index = lax.axis_index("box")
    plane_count = previous.shape[1]
    column_count = previous.shape[2]
    depth_count = previous.shape[3]
    length_all = plane_count * pencils
    segment_count = neighbor.shape[2]
    segment_length = length_all // segment_count
    length_table = sine_table(length_all)
    width_table = sine_table(column_count)
    depth_table = sine_table(depth_count)
    length_eigen = eigen_values(length_all)
    width_eigen = eigen_values(column_count)
    depth_eigen = eigen_values(depth_count)
    forcing = previous[0].astype(jnp.float32) + source[0].astype(jnp.float32)
    positions = jnp.arange(plane_count, dtype=jnp.int32)
    global_planes = pencil_index * plane_count + positions
    segment_hit = (global_planes // segment_length)[:, None] == jnp.arange(
        segment_count, dtype=jnp.int32
    )[None, :]
    own_lists = lax.dynamic_index_in_dim(neighbor, box_index, 0, keepdims=False)
    own_depths = lax.dynamic_index_in_dim(depth, box_index, 0, keepdims=False)
    donor_box = jnp.sum(jnp.where(segment_hit[None], own_lists[:, None, :], 0), axis=2)
    donor_depth = jnp.sum(jnp.where(segment_hit[None], own_depths[:, None, :], 0), axis=2)
    end_planes = ((global_planes == 0) | (global_planes == length_all - 1)).astype(jnp.float32)[
        :, None, None
    ]
    wall_local = wall[0]
    current = previous[0]
    solved = None
    for iteration in range(ITERS):
        iterate = current.astype(jnp.float32)
        high_band = current[:, column_count - 1 - W : column_count - 1, :][:, ::-1, :]
        low_band = current[:, 1 : W + 1, :]
        export = jnp.concatenate([high_band, low_band], axis=1)
        gathered = lax.all_gather(export, "box", axis=0, tiled=True)
        low_import = gathered[donor_box[0] * plane_count + positions, donor_depth[0] - 1, :]
        high_import = gathered[donor_box[1] * plane_count + positions, W + donor_depth[1] - 1, :]
        low_ghost = jnp.where(
            wall_local[0][:, None] == 1, REFLECT * iterate[:, 0, :], low_import.astype(jnp.float32)
        )
        high_ghost = jnp.where(
            wall_local[1][:, None] == 1,
            REFLECT * iterate[:, column_count - 1, :],
            high_import.astype(jnp.float32),
        )
        boundary = jnp.zeros_like(iterate)
        boundary = boundary.at[:, 0, :].add(low_ghost)
        boundary = boundary.at[:, column_count - 1, :].add(high_ghost)
        boundary = boundary + end_planes * (REFLECT * iterate)
        boundary = boundary.at[:, :, 0].add(REFLECT * iterate[:, :, 0])
        boundary = boundary.at[:, :, depth_count - 1].add(REFLECT * iterate[:, :, depth_count - 1])
        right_side = (forcing + TIMESTEP * boundary).astype(jnp.bfloat16)
        first_pass = jnp.einsum(
            "xyz,zk->xyk", right_side, depth_table, preferred_element_type=jnp.float32
        ).astype(jnp.bfloat16)
        second_pass = jnp.einsum(
            "xyz,yk->xkz", first_pass, width_table, preferred_element_type=jnp.float32
        ).astype(jnp.bfloat16)
        spread = lax.all_to_all(second_pass, "pencil", split_axis=1, concat_axis=0, tiled=True)
        width_part = spread.shape[1]
        width_slice = lax.dynamic_slice_in_dim(width_eigen, pencil_index * width_part, width_part)
        spectrum = 1.0 + TIMESTEP * (
            length_eigen[:, None, None] + width_slice[None, :, None] + depth_eigen[None, None, :]
        )
        third_pass = jnp.einsum(
            "xyz,xk->kyz", spread, length_table, preferred_element_type=jnp.float32
        )
        fourth_pass = (third_pass / spectrum).astype(jnp.bfloat16)
        fifth_pass = jnp.einsum(
            "xyz,xk->kyz", fourth_pass, length_table, preferred_element_type=jnp.float32
        ).astype(jnp.bfloat16)
        returned = lax.all_to_all(fifth_pass, "pencil", split_axis=0, concat_axis=1, tiled=True)
        sixth_pass = jnp.einsum(
            "xyz,yk->xkz", returned, width_table, preferred_element_type=jnp.float32
        ).astype(jnp.bfloat16)
        solved = jnp.einsum(
            "xyz,zk->xyk", sixth_pass, depth_table, preferred_element_type=jnp.float32
        )
        current = solved.astype(jnp.bfloat16)
    return solved[None]


def solution(mesh):
    placed = (
        P("box", "pencil", None, None),
        P("box", "pencil", None, None),
        P(),
        P(),
        P("box", None, "pencil"),
    )
    return jax.shard_map(
        shards,
        mesh=mesh,
        in_specs=placed,
        out_specs=P("box", "pencil", None, None),
        check_vma=False,
    )
```

profile of v0, /device:TPU:1, one launch (start us, length us, event | category | flops | bytes accessed | tf_op | source)
XLA Modules:
  0.0 454.8 jit_solution(6380604464187133774)
XLA Ops:
  10.2 4.2 bitcast_convert_fusion
  14.5 77.5 %all-gather.3.cloned.1.call-done = bf16[1024,16,128]{2,1,0:T(8,128)(2,1)} async-done(((bf16[32,16,128]{2,1,0:T(8,128)(2,1)}), bf16[1024,16,128]{2,1,0:T(8,128)(2,1)}) %all-gather.3.cloned.1.call-update) | async-done | bytes 4194320 | tf_op jit(solution)/shard_map/all_gather | solution.py:60
  95.9 2.4 scatter-add.26
  99.9 3.0 multiply_add_fusion.2
  104.9 2.6 fusion.3
  107.5 10.9 %scatter-add.30 = f32[32,256,128]{2,1,0:T(8,128)} dynamic-update-slice(f32[32,256,128]{2,1,0:T(8,128)} %copy-done.1, f32[32,256,1]{2,1,0:T(8,128)} %fusion.3, s32[]{:T(128)} %constant.259.clone.1, s32[]{:T(128)} %constant.259.clone.1, s32[]{:T(128)} %constant.259.clone.1) | dynamic-update-slice | bytes 65540 | tf_op jit(solution)/shard_map/scatter-add | solution.py:75
  118.4 7.7 %fusion.2 = f32[32,256,1]{2,1,0:T(8,128)} fusion(f32[32,256,128]{2,1,0:T(8,128)} %bitcast_convert_fusion, f32[32,256,128]{2,1,0:T(8,128)} %scatter-add.30), kind=kLoop, calls=%fused_computation.9 | loop fusion | flops 16384 | bytes 98304 | tf_op jit(solution)/shard_map/add | solution.py:76
  126.1 13.0 %scatter-add.31 = f32[32,256,128]{2,1,0:T(8,128)} dynamic-update-slice(f32[32,256,128]{2,1,0:T(8,128)} %scatter-add.30, f32[32,256,1]{2,1,0:T(8,128)} %fusion.2, s32[]{:T(128)} %constant.259.clone.1, s32[]{:T(128)} %constant.259.clone.1, s32[]{:T(128)} %constant.270.clone.1) | dynamic-update-slice | bytes 65540 | tf_op jit(solution)/shard_map/scatter-add | solution.py:76
  139.1 6.7 %convert_bitcast_fusion.1 = bf16[32,256,128]{2,1,0:T(8,128)(2,1)} fusion(f32[32,256,128]{2,1,0:T(8,128)} %scatter-add.31, bf16[1,32,256,128]{3,2,1,0:T(8,128)(2,1)} %param.22, f32[256]{0:T(256)S(1)} %get-tuple-element.119, f32[256]{0:T(256)S(1)} %get-tuple-element.120, f32[128]{0:T(128)S(1)} %get-tuple-element.121, f32[128]{0:T(128)S(1)} %get-tuple-element.122, ...), kind=kOutput, calls=%fused_computation.38 | convolution fusion | flops 814022656 | bytes 10488832 | tf_op jit(solution)/shard_map/xyz,yk->xkz/dot_general | solution.py:81
  145.8 4.3 copy.28
  150.1 8.5 %all-to-all-start = ((bf16[32,256,128]{2,0,1:T(8,128)(2,1)}), bf16[32,256,128]{2,0,1:T(8,128)(2,1)}, u32[]{:S(2)}, u32[]{:S(2)}) async-start(bf16[32,256,128]{2,0,1:T(8,128)(2,1)} %copy.28), calls=%async_computation | async-start | bytes 4194304 | tf_op jit(solution)/shard_map/all_to_all | solution.py:84
  159.3 25.6 %all-to-all-done = bf16[32,256,128]{2,0,1:T(8,128)(2,1)} async-done(((bf16[32,256,128]{2,0,1:T(8,128)(2,1)}), bf16[32,256,128]{2,0,1:T(8,128)(2,1)}, u32[]{:S(2)}, u32[]{:S(2)}) %all-to-all-start) | async-done | bytes 2097184 | tf_op jit(solution)/shard_map/all_to_all | solution.py:84
  184.9 3.7 copy.30
  188.6 6.9 %fusion.32 = bf16[256,32,128]{2,0,1:T(8,128)(2,1)} fusion(f32[128]{0:T(128)S(1)} %multiply_subtract_fusion.1, f32[256,32]{0,1:T(8,128)S(1)} %broadcast_add_fusion, bf16[256,32,128]{2,1,0:T(8,128)(2,1)} %bitcast.148, f32[256]{0:T(256)S(1)} %get-tuple-element.119, f32[256]{0:T(256)S(1)} %get-tuple-element.120), kind=kOutput, calls=%fused_computation.47 | convolution fusion | flops 1080557568 | bytes 4229632 | tf_op jit(solution)/shard_map/xyz,xk->kyz/dot_general | solution.py:94
  195.4 2.9 copy.32
  198.4 29.8 %all_to_all.72 = bf16[256,32,128]{2,1,0:T(8,128)(2,1)S(1)} all-to-all(bf16[256,32,128]{2,1,0:T(8,128)(2,1)S(1)} %copy.32), channel_id=1, replica_groups=mesh['box'=32,'pencil'=8] {'pencil'}, dimensions={0} | all-to-all | bytes 4194304 | tf_op jit(solution)/shard_map/all_to_all | solution.py:97
  228.2 2.0 copy.33
  230.1 6.5 %fusion.171 = (f32[32,256,128]{2,1,0:T(8,128)}, bf16[32,256,128]{2,1,0:T(8,128)(2,1)}) fusion(f32[128]{0:T(128)S(1)} %get-tuple-element.121, f32[128]{0:T(128)S(1)} %get-tuple-element.122, bf16[32,256,128]{2,1,0:T(8,128)(2,1)} %bitcast.142, f32[256]{0:T(256)S(1)} %get-tuple-element.119, f32[256]{0:T(256)S(1)} %get-tuple-element.120), kind=kOutput, calls=%fused_computation.160 | convolution fusion | flops 808779776 | bytes 8391680 | tf_op jit(solution)/shard_map/xyz,zk->xyk/dot_general | solution.py:101
  238.4 73.6 %all-gather.5.cloned.1.call-done = bf16[1024,16,128]{2,1,0:T(8,128)(2,1)} async-done(((bf16[32,16,128]{2,1,0:T(8,128)(2,1)}), bf16[1024,16,128]{2,1,0:T(8,128)(2,1)}) %all-gather.5.cloned.1.call-update) | async-done | bytes 4194320 | tf_op jit(solution)/shard_map/all_gather | solution.py:60
  316.0 2.4 scatter-add.34
  320.0 3.7 multiply_add_fusion
  325.7 2.6 fusion.1
  328.3 10.9 %scatter-add.36 = f32[32,256,128]{2,1,0:T(8,128)} dynamic-update-slice(f32[32,256,128]{2,1,0:T(8,128)} %copy-done, f32[32,256,1]{2,1,0:T(8,128)} %fusion.1, s32[]{:T(128)} %constant.259.clone.1, s32[]{:T(128)} %constant.259.clone.1, s32[]{:T(128)} %constant.259.clone.1) | dynamic-update-slice | bytes 65540 | tf_op jit(solution)/shard_map/scatter-add | solution.py:75
  339.2 7.7 %fusion = f32[32,256,1]{2,1,0:T(8,128)} fusion(f32[32,256,128]{2,1,0:T(8,128)} %get-tuple-element.115, f32[32,256,128]{2,1,0:T(8,128)} %scatter-add.36), kind=kLoop, calls=%fused_computation.5 | loop fusion | flops 16384 | bytes 98304 | tf_op jit(solution)/shard_map/add | solution.py:76
  346.9 13.0 %scatter-add.39 = f32[32,256,128]{2,1,0:T(8,128)} dynamic-update-slice(f32[32,256,128]{2,1,0:T(8,128)} %scatter-add.36, f32[32,256,1]{2,1,0:T(8,128)} %fusion, s32[]{:T(128)} %constant.259.clone.1, s32[]{:T(128)} %constant.259.clone.1, s32[]{:T(128)} %constant.270.clone.1) | dynamic-update-slice | bytes 65540 | tf_op jit(solution)/shard_map/scatter-add | solution.py:76
  359.9 6.7 %convert_bitcast_fusion = bf16[32,256,128]{2,1,0:T(8,128)(2,1)} fusion(f32[32,256,128]{2,1,0:T(8,128)} %scatter-add.39, bf16[1,32,256,128]{3,2,1,0:T(8,128)(2,1)} %param.22, f32[256]{0:T(256)S(1)} %get-tuple-element.119, f32[256]{0:T(256)S(1)} %get-tuple-element.120, f32[128]{0:T(128)S(1)} %get-tuple-element.121, f32[128]{0:T(128)S(1)} %get-tuple-element.122, ...), kind=kOutput, calls=%fused_computation.33 | convolution fusion | flops 814022656 | bytes 10488832 | tf_op jit(solution)/shard_map/xyz,yk->xkz/dot_general | solution.py:81
  366.6 2.9 copy.34
  369.5 34.7 %all_to_all.73 = bf16[32,256,128]{2,0,1:T(8,128)(2,1)S(1)} all-to-all(bf16[32,256,128]{2,0,1:T(8,128)(2,1)S(1)} %copy.34), channel_id=1, replica_groups=mesh['box'=32,'pencil'=8] {'pencil'}, dimensions={1} | all-to-all | bytes 4194304 | tf_op jit(solution)/shard_map/all_to_all | solution.py:84
  405.0 5.2 %fusion.31 = bf16[256,32,128]{2,0,1:T(8,128)(2,1)} fusion(f32[128]{0:T(128)S(1)} %multiply_subtract_fusion.1, f32[256,32]{0,1:T(8,128)S(1)} %broadcast_add_fusion, bf16[256,32,128]{2,1,0:T(8,128)(2,1)S(1)} %bitcast.147, f32[256]{0:T(256)S(1)} %get-tuple-element.119, f32[256]{0:T(256)S(1)} %get-tuple-element.120), kind=kOutput, calls=%fused_computation.46 | convolution fusion | flops 1080557568 | bytes 4229632 | tf_op jit(solution)/shard_map/xyz,xk->kyz/dot_general | solution.py:94
  410.2 2.9 copy.38
  413.2 29.7 %all_to_all.74 = bf16[256,32,128]{2,1,0:T(8,128)(2,1)S(1)} all-to-all(bf16[256,32,128]{2,1,0:T(8,128)(2,1)S(1)} %copy.38), channel_id=1, replica_groups=mesh['box'=32,'pencil'=8] {'pencil'}, dimensions={0} | all-to-all | bytes 4194304 | tf_op jit(solution)/shard_map/all_to_all | solution.py:97
  443.5 4.2 convolution_bitcast_fusion
  (47 shorter events, 22.5 us)
Async XLA Ops:
  6.5 85.4 %all-gather.3.cloned.1.call-start = ((), (), s32[]{:S(2)}) async-start(), calls=%async_computation.4 | async-start | bytes 4325376 | tf_op jit(solution)/shard_map/all_gather | solution.py:60
  10.2 89.7 %copy-start.4 = (bf16[1,32,256,128]{3,2,1,0:T(8,128)(2,1)S(1)}, bf16[1,32,256,128]{3,2,1,0:T(8,128)(2,1)}, u32[]{:S(2)}) copy-start(bf16[1,32,256,128]{3,2,1,0:T(8,128)(2,1)} %param.21) | copy-start | bytes 6291460
  99.9 5.0 %copy-start.3 = (f32[32,256,128]{2,1,0:T(8,128)S(1)}, f32[32,256,128]{2,1,0:T(8,128)}, u32[]{:S(2)}) copy-start(f32[32,256,128]{2,1,0:T(8,128)} %bitcast_convert_fusion) | copy-start | bytes 12582916
  103.0 2.0 copy-start.1
  150.1 34.8 %all-to-all-start = ((bf16[32,256,128]{2,0,1:T(8,128)(2,1)}), bf16[32,256,128]{2,0,1:T(8,128)(2,1)}, u32[]{:S(2)}, u32[]{:S(2)}) async-start(bf16[32,256,128]{2,0,1:T(8,128)(2,1)} %copy.28), calls=%async_computation | async-start | bytes 4194304 | tf_op jit(solution)/shard_map/all_to_all | solution.py:84
  158.6 153.5 %all-gather.5.cloned.1.call-start = ((), (), s32[]{:S(2)}) async-start(), calls=%async_computation.5 | async-start | bytes 4325376 | tf_op jit(solution)/shard_map/all_gather | solution.py:60
  320.0 5.7 %copy-start.2 = (f32[32,256,128]{2,1,0:T(8,128)S(1)}, f32[32,256,128]{2,1,0:T(8,128)}, u32[]{:S(2)}) copy-start(f32[32,256,128]{2,1,0:T(8,128)} %get-tuple-element.115) | copy-start | bytes 12582916
  323.7 2.0 copy-start
Sparse Core Ops, SparseCore 0:
  9.9 81.9 all-gather.2
  238.5 73.4 all-gather.4
where the time goes:
time: 464 us; the launch traced here: 455 us
  waiting for transfers between devices  177 us (38%)
  blocking collectives  94.1 us (20%)
  local copies, waits for them, and re-layouts  88.9 us (19%)
  matrix products  36.3 us (8%)
  other arithmetic  36.1 us (8%)
  between operations  13.8 us (3%)
  starting transfers between devices  8.93 us (2%)
    all_gather x2, waiting for transfers between devices, shards(): gathered = lax.all_gather(export, 'box', axis=0, tiled=True)  151 us
    all_to_all x2, blocking collectives, shards(): lax.all_to_all(fifth_pass, 'pencil', split_axis=0, concat_axis=1, tiled=T...  59.4 us
    all_to_all x1, blocking collectives, shards(): lax.all_to_all(second_pass, 'pencil', split_axis=1, concat_axis=0, tiled=...  34.7 us
    scatter-add x2, local copies, waits for them, and re-layouts, shards(): boundary.at[:, :, depth_count - 1]  26 us
    all_to_all x1, waiting for transfers between devices, shards(): lax.all_to_all(second_pass, 'pencil', split_axis=1, concat_axis=0, tiled=...  25.6 us
    scatter-add x2, local copies, waits for them, and re-layouts, shards(): boundary = boundary.at[:, :, 0].add(REFLECT * iterate[:, :, 0])  21.9 us
    add x2, other arithmetic, shards(): boundary.at[:, :, depth_count - 1]  15.3 us
    dot_general x2, matrix products, shards(): jnp.einsum('xyz,yk->xkz', first_pass, width_table, preferred_element_type...  13.4 us
  transfers between devices with their start and end apart: 3, of which 3 were waited for; matrix products, arithmetic and copies ran while one was open for 1% of the time, Pallas kernels for 0%

commit v1 on v0

--- a/solution.py
+++ b/solution.py
@@ -57,7 +57,9 @@
         high_band = current[:, column_count - 1 - W : column_count - 1, :][:, ::-1, :]
         low_band = current[:, 1 : W + 1, :]
         export = jnp.concatenate([high_band, low_band], axis=1)
-        gathered = lax.all_gather(export, "box", axis=0, tiled=True)
+        gathered = jnp.concatenate(
+            lax.all_to_all(jnp.stack([export] * lax.axis_size("box")), "box", 0, 0), axis=0
+        )
         low_import = gathered[donor_box[0] * plane_count + positions, donor_depth[0] - 1, :]
         high_import = gathered[donor_box[1] * plane_count + positions, W + donor_depth[1] - 1, :]
         low_ghost = jnp.where(

time: 464 us -> 499 us (1.075)
  blocking collectives: 94.1 us -> 190 us
  waiting for transfers between devices: 177 us -> 116 us
  starting transfers between devices: 8.93 us -> 22.5 us
  between operations: 13.8 us -> 0.44 us
    all_gather x2 -> x0, waiting for transfers between devices: 151 us -> none  [shards(): gathered = lax.all_gather(export, 'box', axis=0, tiled=True)]
    all_to_all x0 -> x1, blocking collectives: none -> 97.3 us  [shards(): lax.all_to_all(jnp.stack([export] * lax.axis_size('box')), 'box', 0, 0)]
    all_to_all x0 -> x1, waiting for transfers between devices: none -> 89.6 us  [shards(): lax.all_to_all(jnp.stack([export] * lax.axis_size('box')), 'box', 0, 0)]
    all_to_all x0 -> x1, starting transfers between devices: none -> 12.1 us  [shards(): lax.all_to_all(jnp.stack([export] * lax.axis_size('box')), 'box', 0, 0)]
  transfers between devices with their start and end apart: 3 -> 2, of which waited for: 3 -> 2; matrix products, arithmetic and copies ran while one was open for 1% -> 1% of each run, Pallas kernels for 0% -> 0%
where the time goes in v1:
time: 499 us; the launch traced here: 489 us
  blocking collectives  190 us (38%)
  waiting for transfers between devices  116 us (23%)
  local copies, waits for them, and re-layouts  92.2 us (18%)
  matrix products  36.3 us (7%)
  other arithmetic  32.2 us (6%)
  starting transfers between devices  22.5 us (5%)
    all_to_all x1, blocking collectives, shards(): lax.all_to_all(jnp.stack([export] * lax.axis_size('box')), 'box', 0, 0)  97.3 us
    all_to_all x1, waiting for transfers between devices, shards(): lax.all_to_all(jnp.stack([export] * lax.axis_size('box')), 'box', 0, 0)  89.6 us
    all_to_all x2, blocking collectives, shards(): lax.all_to_all(fifth_pass, 'pencil', split_axis=0, concat_axis=1, tiled=T...  59.2 us
    all_to_all x1, blocking collectives, shards(): lax.all_to_all(second_pass, 'pencil', split_axis=1, concat_axis=0, tiled=...  33.4 us
    scatter-add x2, local copies, waits for them, and re-layouts, shards(): boundary.at[:, :, depth_count - 1]  26 us
    all_to_all x1, waiting for transfers between devices, shards(): lax.all_to_all(second_pass, 'pencil', split_axis=1, concat_axis=0, tiled=...  26 us
    scatter-add x2, local copies, waits for them, and re-layouts, shards(): boundary = boundary.at[:, :, 0].add(REFLECT * iterate[:, :, 0])  21.9 us
    add x2, other arithmetic, shards(): boundary.at[:, :, depth_count - 1]  15.3 us
  transfers between devices with their start and end apart: 2, of which 2 were waited for; matrix products, arithmetic and copies ran while one was open for 1% of the time, Pallas kernels for 0%

profile of v1, /device:TPU:1, one launch (start us, length us, event | category | flops | bytes accessed | tf_op | source)
XLA Modules:
  0.0 489.3 jit_solution(10438752862346802182)
XLA Ops:
  1.1 3.0 stack.4
  4.1 12.1 %all-to-all-start = ((bf16[32,32,16,128]{3,2,1,0:T(8,128)(2,1)}), bf16[32,32,16,128]{3,2,1,0:T(8,128)(2,1)}, u32[]{:S(2)}, u32[]{:S(2)}) async-start(bf16[32,32,16,128]{3,2,1,0:T(8,128)(2,1)} %stack.4), calls=%async_computation | async-start | bytes 8388608 | tf_op jit(solution)/shard_map/all_to_all | solution.py:61
  19.1 89.6 %all-to-all-done = bf16[32,32,16,128]{3,2,1,0:T(8,128)(2,1)} async-done(((bf16[32,32,16,128]{3,2,1,0:T(8,128)(2,1)}), bf16[32,32,16,128]{3,2,1,0:T(8,128)(2,1)}, u32[]{:S(2)}, u32[]{:S(2)}) %all-to-all-start) | async-done | bytes 4194336 | tf_op jit(solution)/shard_map/all_to_all | solution.py:61
  112.6 2.5 scatter-add.26
  116.7 3.0 multiply_add_fusion.2
  121.8 2.6 fusion.3
  124.4 10.9 %scatter-add.30 = f32[32,256,128]{2,1,0:T(8,128)} dynamic-update-slice(f32[32,256,128]{2,1,0:T(8,128)} %copy-done.1, f32[32,256,1]{2,1,0:T(8,128)} %fusion.3, s32[]{:T(128)} %constant.259.clone.1, s32[]{:T(128)} %constant.259.clone.1, s32[]{:T(128)} %constant.259.clone.1) | dynamic-update-slice | bytes 65540 | tf_op jit(solution)/shard_map/scatter-add | solution.py:77
  135.3 7.7 %fusion.2 = f32[32,256,1]{2,1,0:T(8,128)} fusion(f32[32,256,128]{2,1,0:T(8,128)} %bitcast_convert_fusion, f32[32,256,128]{2,1,0:T(8,128)} %scatter-add.30), kind=kLoop, calls=%fused_computation.9 | loop fusion | flops 16384 | bytes 98304 | tf_op jit(solution)/shard_map/add | solution.py:78
  143.0 13.0 %scatter-add.31 = f32[32,256,128]{2,1,0:T(8,128)} dynamic-update-slice(f32[32,256,128]{2,1,0:T(8,128)} %scatter-add.30, f32[32,256,1]{2,1,0:T(8,128)} %fusion.2, s32[]{:T(128)} %constant.259.clone.1, s32[]{:T(128)} %constant.259.clone.1, s32[]{:T(128)} %constant.270.clone.1) | dynamic-update-slice | bytes 65540 | tf_op jit(solution)/shard_map/scatter-add | solution.py:78
  156.0 6.7 %convert_bitcast_fusion.1 = bf16[32,256,128]{2,1,0:T(8,128)(2,1)} fusion(f32[32,256,128]{2,1,0:T(8,128)} %scatter-add.31, bf16[1,32,256,128]{3,2,1,0:T(8,128)(2,1)} %param.22, f32[256]{0:T(256)S(1)} %get-tuple-element.119, f32[256]{0:T(256)S(1)} %get-tuple-element.120, f32[128]{0:T(128)S(1)} %get-tuple-element.121, f32[128]{0:T(128)S(1)} %get-tuple-element.122, ...), kind=kOutput, calls=%fused_computation.38 | convolution fusion | flops 814022656 | bytes 10488832 | tf_op jit(solution)/shard_map/xyz,yk->xkz/dot_general | solution.py:83
  162.7 4.3 copy.28
  167.0 10.4 %all-to-all-start.1 = ((bf16[32,256,128]{2,0,1:T(8,128)(2,1)}), bf16[32,256,128]{2,0,1:T(8,128)(2,1)}, u32[]{:S(2)}, u32[]{:S(2)}) async-start(bf16[32,256,128]{2,0,1:T(8,128)(2,1)} %copy.28), calls=%async_computation.1 | async-start | bytes 4194304 | tf_op jit(solution)/shard_map/all_to_all | solution.py:86
  177.7 26.0 %all-to-all-done.1 = bf16[32,256,128]{2,0,1:T(8,128)(2,1)} async-done(((bf16[32,256,128]{2,0,1:T(8,128)(2,1)}), bf16[32,256,128]{2,0,1:T(8,128)(2,1)}, u32[]{:S(2)}, u32[]{:S(2)}) %all-to-all-start.1) | async-done | bytes 2097184 | tf_op jit(solution)/shard_map/all_to_all | solution.py:86
  203.7 3.7 copy.30
  207.4 6.9 %fusion.32 = bf16[256,32,128]{2,0,1:T(8,128)(2,1)} fusion(f32[128]{0:T(128)S(1)} %multiply_subtract_fusion.1, f32[256,32]{0,1:T(8,128)S(1)} %broadcast_add_fusion, bf16[256,32,128]{2,1,0:T(8,128)(2,1)} %bitcast.152, f32[256]{0:T(256)S(1)} %get-tuple-element.119, f32[256]{0:T(256)S(1)} %get-tuple-element.120), kind=kOutput, calls=%fused_computation.47 | convolution fusion | flops 1080557568 | bytes 4229632 | tf_op jit(solution)/shard_map/xyz,xk->kyz/dot_general | solution.py:96
  214.2 2.9 copy.32
  217.2 29.6 %all_to_all.82 = bf16[256,32,128]{2,1,0:T(8,128)(2,1)S(1)} all-to-all(bf16[256,32,128]{2,1,0:T(8,128)(2,1)S(1)} %copy.32), channel_id=1, replica_groups=mesh['box'=32,'pencil'=8] {'pencil'}, dimensions={0} | all-to-all | bytes 4194304 | tf_op jit(solution)/shard_map/all_to_all | solution.py:99
  248.7 6.5 %fusion.171 = (f32[32,256,128]{2,1,0:T(8,128)}, bf16[32,256,128]{2,1,0:T(8,128)(2,1)}) fusion(f32[128]{0:T(128)S(1)} %get-tuple-element.121, f32[128]{0:T(128)S(1)} %get-tuple-element.122, bf16[32,256,128]{2,1,0:T(8,128)(2,1)} %bitcast.144, f32[256]{0:T(256)S(1)} %get-tuple-element.119, f32[256]{0:T(256)S(1)} %get-tuple-element.120), kind=kOutput, calls=%fused_computation.160 | convolution fusion | flops 808779776 | bytes 8391680 | tf_op jit(solution)/shard_map/xyz,zk->xyk/dot_general | solution.py:103
  257.3 97.3 %all_to_all.83 = bf16[32,32,16,128]{3,2,1,0:T(8,128)(2,1)} all-to-all(bf16[32,32,16,128]{3,2,1,0:T(8,128)(2,1)S(1)} %stack.5), channel_id=1, replica_groups=mesh['box'=32,'pencil'=8] {'box'}, dimensions={0} | all-to-all | bytes 8388608 | tf_op jit(solution)/shard_map/all_to_all | solution.py:61
  358.5 2.4 scatter-add.34
  362.6 3.7 multiply_add_fusion
  368.3 2.6 fusion.1
  370.9 10.9 %scatter-add.36 = f32[32,256,128]{2,1,0:T(8,128)} dynamic-update-slice(f32[32,256,128]{2,1,0:T(8,128)} %copy-done, f32[32,256,1]{2,1,0:T(8,128)} %fusion.1, s32[]{:T(128)} %constant.259.clone.1, s32[]{:T(128)} %constant.259.clone.1, s32[]{:T(128)} %constant.259.clone.1) | dynamic-update-slice | bytes 65540 | tf_op jit(solution)/shard_map/scatter-add | solution.py:77
  381.8 7.7 %fusion = f32[32,256,1]{2,1,0:T(8,128)} fusion(f32[32,256,128]{2,1,0:T(8,128)} %get-tuple-element.115, f32[32,256,128]{2,1,0:T(8,128)} %scatter-add.36), kind=kLoop, calls=%fused_computation.5 | loop fusion | flops 16384 | bytes 98304 | tf_op jit(solution)/shard_map/add | solution.py:78
  389.5 13.0 %scatter-add.39 = f32[32,256,128]{2,1,0:T(8,128)} dynamic-update-slice(f32[32,256,128]{2,1,0:T(8,128)} %scatter-add.36, f32[32,256,1]{2,1,0:T(8,128)} %fusion, s32[]{:T(128)} %constant.259.clone.1, s32[]{:T(128)} %constant.259.clone.1, s32[]{:T(128)} %constant.270.clone.1) | dynamic-update-slice | bytes 65540 | tf_op jit(solution)/shard_map/scatter-add | solution.py:78
  402.5 6.7 %convert_bitcast_fusion = bf16[32,256,128]{2,1,0:T(8,128)(2,1)} fusion(f32[32,256,128]{2,1,0:T(8,128)} %scatter-add.39, bf16[1,32,256,128]{3,2,1,0:T(8,128)(2,1)} %param.22, f32[256]{0:T(256)S(1)} %get-tuple-element.119, f32[256]{0:T(256)S(1)} %get-tuple-element.120, f32[128]{0:T(128)S(1)} %get-tuple-element.121, f32[128]{0:T(128)S(1)} %get-tuple-element.122, ...), kind=kOutput, calls=%fused_computation.33 | convolution fusion | flops 814022656 | bytes 10488832 | tf_op jit(solution)/shard_map/xyz,yk->xkz/dot_general | solution.py:83
  409.2 2.9 copy.34
  412.1 33.4 %all_to_all.84 = bf16[32,256,128]{2,0,1:T(8,128)(2,1)S(1)} all-to-all(bf16[32,256,128]{2,0,1:T(8,128)(2,1)S(1)} %copy.34), channel_id=1, replica_groups=mesh['box'=32,'pencil'=8] {'pencil'}, dimensions={1} | all-to-all | bytes 4194304 | tf_op jit(solution)/shard_map/all_to_all | solution.py:86
  446.4 5.2 %fusion.31 = bf16[256,32,128]{2,0,1:T(8,128)(2,1)} fusion(f32[128]{0:T(128)S(1)} %multiply_subtract_fusion.1, f32[256,32]{0,1:T(8,128)S(1)} %broadcast_add_fusion, bf16[256,32,128]{2,1,0:T(8,128)(2,1)S(1)} %bitcast.151, f32[256]{0:T(256)S(1)} %get-tuple-element.119, f32[256]{0:T(256)S(1)} %get-tuple-element.120), kind=kOutput, calls=%fused_computation.46 | convolution fusion | flops 1080557568 | bytes 4229632 | tf_op jit(solution)/shard_map/xyz,xk->kyz/dot_general | solution.py:96
  451.6 2.9 copy.38
  454.5 29.6 %all_to_all.85 = bf16[256,32,128]{2,1,0:T(8,128)(2,1)S(1)} all-to-all(bf16[256,32,128]{2,1,0:T(8,128)(2,1)S(1)} %copy.38), channel_id=1, replica_groups=mesh['box'=32,'pencil'=8] {'pencil'}, dimensions={0} | all-to-all | bytes 4194304 | tf_op jit(solution)/shard_map/all_to_all | solution.py:99
  484.8 4.2 convolution_bitcast_fusion
  (52 shorter events, 24.6 us)
Async XLA Ops:
  4.0 12.2 %copy-start.5 = (s32[32,2,16]{0,2,1:T(8,128)S(1)}, s32[32,2,16]{0,2,1:T(8,128)}, u32[]{:S(2)}) copy-start(s32[32,2,16]{0,2,1:T(8,128)} %param.24) | copy-start | bytes 12292
  4.0 12.2 %copy-start.6 = (s32[32,2,16]{0,2,1:T(8,128)S(1)}, s32[32,2,16]{0,2,1:T(8,128)}, u32[]{:S(2)}) copy-start(s32[32,2,16]{0,2,1:T(8,128)} %param.23) | copy-start | bytes 12292
  4.1 12.5 %copy-start.7 = (s32[1,2,32]{2,1,0:T(2,128)S(1)}, s32[1,2,32]{2,1,0:T(2,128)}, u32[]{:S(2)}) copy-start(s32[1,2,32]{2,1,0:T(2,128)} %param.25) | copy-start | bytes 772
  4.1 12.6 %copy-start.4 = (bf16[1,32,256,128]{3,2,1,0:T(8,128)(2,1)S(1)}, bf16[1,32,256,128]{3,2,1,0:T(8,128)(2,1)}, u32[]{:S(2)}) copy-start(bf16[1,32,256,128]{3,2,1,0:T(8,128)(2,1)} %param.21) | copy-start | bytes 6291460
  4.1 104.7 %all-to-all-start = ((bf16[32,32,16,128]{3,2,1,0:T(8,128)(2,1)}), bf16[32,32,16,128]{3,2,1,0:T(8,128)(2,1)}, u32[]{:S(2)}, u32[]{:S(2)}) async-start(bf16[32,32,16,128]{3,2,1,0:T(8,128)(2,1)} %stack.4), calls=%async_computation | async-start | bytes 8388608 | tf_op jit(solution)/shard_map/all_to_all | solution.py:61
  116.7 5.1 %copy-start.3 = (f32[32,256,128]{2,1,0:T(8,128)S(1)}, f32[32,256,128]{2,1,0:T(8,128)}, u32[]{:S(2)}) copy-start(f32[32,256,128]{2,1,0:T(8,128)} %bitcast_convert_fusion) | copy-start | bytes 12582916
  119.8 2.0 copy-start.1
  167.0 36.7 %all-to-all-start.1 = ((bf16[32,256,128]{2,0,1:T(8,128)(2,1)}), bf16[32,256,128]{2,0,1:T(8,128)(2,1)}, u32[]{:S(2)}, u32[]{:S(2)}) async-start(bf16[32,256,128]{2,0,1:T(8,128)(2,1)} %copy.28), calls=%async_computation.1 | async-start | bytes 4194304 | tf_op jit(solution)/shard_map/all_to_all | solution.py:86
  362.6 5.7 %copy-start.2 = (f32[32,256,128]{2,1,0:T(8,128)S(1)}, f32[32,256,128]{2,1,0:T(8,128)}, u32[]{:S(2)}) copy-start(f32[32,256,128]{2,1,0:T(8,128)} %get-tuple-element.115) | copy-start | bytes 12582916
  366.3 2.0 copy-start
